TPU v7x, 32 devices: a whole 2x2x4 slice. The times are simulated.
32 devices in a mesh: dp: 8 (over y, x, core), group: 4 (over z).
Axes of the slice: x: 2, y: 2, z: 4, core: 2. Of those that a mesh axis runs over, the one named last changes fastest.
Arguments:
- stream: float32 [8192, 1024], P(('dp', 'group')), may hold values from -6 to 6
- cotangent: float32 [8192, 1024], P(('dp', 'group')), may hold values from -6 to 6
- bounds: int32 [8192, 2], P(('dp', 'group')), may hold values from 0 to 8192, as said below
- joined_proj: float32 [1024, 3072], P(('dp', 'group'))
- out_proj: float32 [1024, 1024], P(('dp', 'group')), may hold values from -3 to 3
- wide_proj: float32 [1024, 5248], P(('dp', 'group')), may hold values from -0.1875 to 0.1875
- down_proj: float32 [1024, 2624], P(('dp', 'group')), may hold values from -0.125 to 0.125
- gain_first: float32 [1024], P(('dp', 'group')), may hold values from 0.5 to 1.5
- gain_second: float32 [1024], P(('dp', 'group')), may hold values from 0.5 to 1.5
- joined_momentum: float32 [1024, 3072], P(('dp', 'group')), may hold values from -6 to 6
- out_momentum: float32 [1024, 1024], P(('dp', 'group')), may hold values from -6 to 6
- wide_momentum: float32 [1024, 5248], P(('dp', 'group')), may hold values from -6 to 6
- down_momentum: float32 [1024, 2624], P(('dp', 'group')), may hold values from -6 to 6
- gain_first_momentum: float32 [1024], P(('dp', 'group')), may hold values from -6 to 6
- gain_second_momentum: float32 [1024], P(('dp', 'group')), may hold values from -6 to 6
- joined_variance: float32 [1024, 3072], P(('dp', 'group')), may hold values from 1 to 100
- out_variance: float32 [1024, 1024], P(('dp', 'group')), may hold values from 1 to 100
- wide_variance: float32 [1024, 5248], P(('dp', 'group')), may hold values from 1 to 100
- down_variance: float32 [1024, 2624], P(('dp', 'group')), may hold values from 1 to 100
- gain_first_variance: float32 [1024], P(('dp', 'group')), may hold values from 1 to 100
- gain_second_variance: float32 [1024], P(('dp', 'group')), may hold values from 1 to 100
Outputs:
- output: float32 [8192, 1024], P(('dp', 'group'))
- stream_grad: float32 [8192, 1024], P(('dp', 'group'))
- joined_grad: float32 [1024, 3072], P(('dp', 'group'))
- out_grad: float32 [1024, 1024], P(('dp', 'group'))
- wide_grad: float32 [1024, 5248], P(('dp', 'group'))
- down_grad: float32 [1024, 2624], P(('dp', 'group'))
- gain_first_grad: float32 [1024], P(('dp', 'group'))
- gain_second_grad: float32 [1024], P(('dp', 'group'))
- joined_new: float32 [1024, 3072], P(('dp', 'group'))
- out_new: float32 [1024, 1024], P(('dp', 'group'))
- wide_new: float32 [1024, 5248], P(('dp', 'group'))
- down_new: float32 [1024, 2624], P(('dp', 'group'))
- gain_first_new: float32 [1024], P(('dp', 'group'))
- gain_second_new: float32 [1024], P(('dp', 'group'))
- joined_momentum_new: float32 [1024, 3072], P(('dp', 'group'))
- out_momentum_new: float32 [1024, 1024], P(('dp', 'group'))
- wide_momentum_new: float32 [1024, 5248], P(('dp', 'group'))
- down_momentum_new: float32 [1024, 2624], P(('dp', 'group'))
- gain_first_momentum_new: float32 [1024], P(('dp', 'group'))
- gain_second_momentum_new: float32 [1024], P(('dp', 'group'))
- joined_variance_new: float32 [1024, 3072], P(('dp', 'group'))
- out_variance_new: float32 [1024, 1024], P(('dp', 'group'))
- wide_variance_new: float32 [1024, 5248], P(('dp', 'group'))
- down_variance_new: float32 [1024, 2624], P(('dp', 'group'))
- gain_first_variance_new: float32 [1024], P(('dp', 'group'))
- gain_second_variance_new: float32 [1024], P(('dp', 'group'))
Inputs may be any that keep to these rules, and one draw needn't show every extreme that they name: `bounds`: each row holds the first token index and one past the last token index of that token's sequence; sequences are contiguous, cover all tokens in order and hold 1 to 1024 tokens, exactly 1024 for one of them, 128 or more for all but the last.
All inputs are finite; a program needn't handle non-finite values.
Results may differ from a plain program's by a relative error of at most 0.018.
Values may be sent and summed in bfloat16 or wider, within the bound.
A program may use at most 320 MiB of HBM per device.

v0:
```python
import math

import jax
import jax.numpy as jnp
from jax import lax
from jax.sharding import PartitionSpec as P

HEAD_DIM = 64
LMAX = 1024
STEP = 4


EPSILON = 1e-05
ROPE_BASE = 160000.0
LEARN_RATE = 0.02
BETA_ONE = 0.9
BETA_TWO = 0.98
ADAM_EPSILON = 1e-06
WEIGHT_DECAY = 0.1
NEG_LARGE = -1e30


def extended(x, sides, width):
    for axis, dim in sides:
        peers, length = (lax.axis_size(axis), x.shape[dim])
        up = [(i, (i + 1) % peers) for i in range(peers - 1)]
        down = [(j, i) for i, j in up]
        last = lax.slice_in_dim(x, length - width, length, axis=dim)
        initial = lax.slice_in_dim(x, 0, width, axis=dim)
        before = lax.ppermute(last, axis, up)
        after = lax.ppermute(initial, axis, down)
        x = jnp.concatenate([before, x, after], axis=dim)
    return x


def normalize(values):
    centred = values - jnp.mean(values, axis=1, keepdims=True)
    row_scale = lax.rsqrt(jnp.mean(centred * centred, axis=1, keepdims=True) + EPSILON)
    return (centred * row_scale, row_scale)


def norm_back(grad_hat, normed, row_scale):
    mean_one = jnp.mean(grad_hat, axis=1, keepdims=True)
    mean_two = jnp.mean(grad_hat * normed, axis=1, keepdims=True)
    return row_scale * (grad_hat - mean_one - normed * mean_two)


def rope_tables(positions):
    half_dim = HEAD_DIM // 2
    freqs = jnp.exp(
        jnp.arange(half_dim, dtype=jnp.float32) * (-2.0 * math.log(ROPE_BASE) / HEAD_DIM)
    )
    angles = positions.astype(jnp.float32)[:, None] * freqs[None, :]
    return (jnp.cos(angles), jnp.sin(angles))


def rotate(values, cosine, sine_table, sign):
    half_dim = values.shape[-1] // 2
    front_half = values[..., :half_dim]
    second = values[..., half_dim:]
    cos_part = cosine[:, None, :]
    sin_part = sine_table[:, None, :] * sign
    return jnp.concatenate(
        [front_half * cos_part - second * sin_part, second * cos_part + front_half * sin_part],
        axis=-1,
    )


def gelu_parts(inner_part):
    cdf_part = 0.5 * (1.0 + lax.erf(inner_part * (1.0 / math.sqrt(2.0))))
    activation = inner_part * cdf_part
    gelu_slope = cdf_part + inner_part * jnp.exp(-0.5 * inner_part * inner_part) * (
        1.0 / math.sqrt(2.0 * math.pi)
    )
    return (activation, gelu_slope)


def score_block(queries, win_keys, key_mask):
    scores = jnp.einsum(
        "rhd,khd->hrk", queries, win_keys, preferred_element_type=jnp.float32
    ) * HEAD_DIM ** (-0.5)
    return jnp.where(key_mask[None], scores, NEG_LARGE)


def attend_forward(queries, win_keys, win_values, key_mask):
    scores = score_block(queries, win_keys, key_mask)
    row_peak = jnp.max(scores, axis=2, keepdims=True)
    sum_exp = jnp.sum(jnp.exp(scores - row_peak), axis=2, keepdims=True)
    log_norm = row_peak + jnp.log(sum_exp)
    prob_round = jnp.exp(scores - log_norm).astype(jnp.bfloat16)
    mixed = jnp.einsum("hrk,khd->rhd", prob_round, win_values, preferred_element_type=jnp.float32)
    return (mixed, log_norm[..., 0])


def attend_backward(queries, win_keys, win_values, key_mask, log_norm, attended, grad_attended):
    scores = score_block(queries, win_keys, key_mask)
    probs = jnp.exp(scores - log_norm[..., None])
    prob_round = probs.astype(jnp.bfloat16)
    grad_prob = jnp.einsum(
        "rhd,khd->hrk", grad_attended, win_values, preferred_element_type=jnp.float32
    )
    row_delta = jnp.sum(grad_attended.astype(jnp.float32) * attended.astype(jnp.float32), axis=2).T
    grad_score = (probs * (grad_prob - row_delta[..., None])).astype(jnp.bfloat16)
    grad_query = jnp.einsum(
        "hrk,khd->rhd", grad_score, win_keys, preferred_element_type=jnp.float32
    ) * HEAD_DIM ** (-0.5)
    grad_key = jnp.einsum(
        "hrk,rhd->khd", grad_score, queries, preferred_element_type=jnp.float32
    ) * HEAD_DIM ** (-0.5)
    grad_value = jnp.einsum(
        "hrk,rhd->khd", prob_round, grad_attended, preferred_element_type=jnp.float32
    )
    return (grad_query, grad_key, grad_value)


def adam_step(weight, gradient, momentum, variance, decay_rate):
    new_momentum = BETA_ONE * momentum + (1.0 - BETA_ONE) * gradient
    new_variance = BETA_TWO * variance + (1.0 - BETA_TWO) * gradient * gradient
    update = (
        new_momentum
        / (1.0 - BETA_ONE**STEP)
        / (jnp.sqrt(new_variance / (1.0 - BETA_TWO**STEP)) + ADAM_EPSILON)
    )
    return (weight - LEARN_RATE * (update + decay_rate * weight), new_momentum, new_variance)


def on_device(
    stream,
    cotangent,
    bounds,
    joined_proj,
    out_proj,
    wide_proj,
    down_proj,
    gain_first,
    gain_second,
    joined_momentum,
    out_momentum,
    wide_momentum,
    down_momentum,
    gain_first_momentum,
    gain_second_momentum,
    joined_variance,
    out_variance,
    wide_variance,
    down_variance,
    gain_first_variance,
    gain_second_variance,
):
    row_count = stream.shape[0]
    width = stream.shape[1]
    heads = width // HEAD_DIM
    masters = (
        joined_proj.astype(jnp.bfloat16),
        out_proj.astype(jnp.bfloat16),
        wide_proj.astype(jnp.bfloat16),
        down_proj.astype(jnp.bfloat16),
        gain_first.astype(jnp.bfloat16),
        gain_second.astype(jnp.bfloat16),
    )
    gathered = (
        lax.all_gather(masters[0], ("dp", "group"), axis=0, tiled=True),
        lax.all_gather(masters[1], ("dp", "group"), axis=0, tiled=True),
        lax.all_gather(masters[2], ("dp", "group"), axis=0, tiled=True),
        lax.all_gather(masters[3], ("dp", "group"), axis=0, tiled=True),
        lax.all_gather(masters[4], ("dp", "group"), axis=0, tiled=True),
        lax.all_gather(masters[5], ("dp", "group"), axis=0, tiled=True),
    )
    joined_half, out_half, wide_half, down_half, gain_one_half, gain_two_half = gathered
    gain_one = gain_one_half.astype(jnp.float32)
    gain_two = gain_two_half.astype(jnp.float32)
    ff_width = down_half.shape[1]
    first_row = lax.axis_index(("dp", "group")) * row_count
    token_index = first_row + jnp.arange(row_count, dtype=jnp.int32)
    seq_starts = bounds[:, 0]
    seq_ends = bounds[:, 1]
    cosine, sine_table = rope_tables(token_index - seq_starts)
    normed_one, scale_one = normalize(stream)
    normed_in = (normed_one * gain_one).astype(jnp.bfloat16)
    joined_act = jnp.dot(normed_in, joined_half, preferred_element_type=jnp.float32)
    queries = rotate(
        joined_act[:, :width].reshape(row_count, heads, HEAD_DIM), cosine, sine_table, 1.0
    ).astype(jnp.bfloat16)
    own_keys = rotate(
        joined_act[:, width : 2 * width].reshape(row_count, heads, HEAD_DIM),
        cosine,
        sine_table,
        1.0,
    )
    pairs = jnp.concatenate(
        [
            own_keys.astype(jnp.bfloat16).reshape(row_count, width),
            joined_act[:, 2 * width :].astype(jnp.bfloat16),
        ],
        axis=1,
    )
    key_span = row_count + 2 * LMAX
    group_block = lax.all_gather(pairs, "group", axis=0, tiled=True)
    padded = extended(group_block, (("dp", 0),), LMAX)
    window = lax.dynamic_slice_in_dim(padded, lax.axis_index("group") * row_count, key_span, 0)
    key_index = first_row - LMAX + jnp.arange(key_span, dtype=jnp.int32)
    key_mask = (key_index[None, :] >= seq_starts[:, None]) & (
        key_index[None, :] < seq_ends[:, None]
    )
    win_keys = window[:, :width].reshape(key_span, heads, HEAD_DIM)
    win_values = window[:, width:].reshape(key_span, heads, HEAD_DIM)
    mixed_parts = []
    norm_parts = []
    for head_start in range(0, heads, 4):
        mixed, log_norm = attend_forward(
            queries[:, head_start : head_start + 4],
            win_keys[:, head_start : head_start + 4],
            win_values[:, head_start : head_start + 4],
            key_mask,
        )
        mixed_parts.append(mixed)
        norm_parts.append(log_norm)
    attended = jnp.concatenate(mixed_parts, axis=1).astype(jnp.bfloat16).reshape(row_count, width)
    residual = stream + jnp.dot(attended, out_half, preferred_element_type=jnp.float32)
    normed_two, scale_two = normalize(residual)
    hidden_in = (normed_two * gain_two).astype(jnp.bfloat16)
    wide_act = jnp.dot(hidden_in, wide_half, preferred_element_type=jnp.float32)
    inner_part = wide_act[:, :ff_width]
    gate_part = wide_act[:, ff_width:]
    activation, gelu_slope = gelu_parts(inner_part)
    gated = (activation * gate_part).astype(jnp.bfloat16)
    output = residual + jnp.einsum(
        "rf,df->rd", gated, down_half, preferred_element_type=jnp.float32
    )
    cot_half = cotangent.astype(jnp.bfloat16)
    down_local = jnp.einsum("rd,rf->df", cot_half, gated, preferred_element_type=jnp.float32)
    grad_gated = jnp.dot(cot_half, down_half, preferred_element_type=jnp.float32)
    grad_wide = jnp.concatenate(
        [grad_gated * gate_part * gelu_slope, grad_gated * activation], axis=1
    ).astype(jnp.bfloat16)
    wide_local = jnp.einsum("rd,rf->df", hidden_in, grad_wide, preferred_element_type=jnp.float32)
    grad_hidden = jnp.einsum("rf,df->rd", grad_wide, wide_half, preferred_element_type=jnp.float32)
    gain_two_local = jnp.sum(grad_hidden * normed_two, axis=0)
    grad_resid = cotangent + norm_back(grad_hidden * gain_two, normed_two, scale_two)
    resid_half = grad_resid.astype(jnp.bfloat16)
    out_local = jnp.einsum("rd,re->de", attended, resid_half, preferred_element_type=jnp.float32)
    grad_attended = jnp.einsum(
        "re,de->rd", resid_half, out_half, preferred_element_type=jnp.float32
    ).astype(jnp.bfloat16)
    attended_heads = attended.reshape(row_count, heads, HEAD_DIM)
    grad_heads = grad_attended.reshape(row_count, heads, HEAD_DIM)
    query_parts = []
    key_parts = []
    value_parts = []
    for part_index, head_start in enumerate(range(0, heads, 4)):
        grad_query, grad_key, grad_value = attend_backward(
            queries[:, head_start : head_start + 4],
            win_keys[:, head_start : head_start + 4],
            win_values[:, head_start : head_start + 4],
            key_mask,
            norm_parts[part_index],
            attended_heads[:, head_start : head_start + 4],
            grad_heads[:, head_start : head_start + 4],
        )
        query_parts.append(grad_query)
        key_parts.append(grad_key)
        value_parts.append(grad_value)
    grad_queries = jnp.concatenate(query_parts, axis=1)
    grad_window = jnp.concatenate(
        [
            jnp.concatenate(key_parts, axis=1).reshape(key_span, width),
            jnp.concatenate(value_parts, axis=1).reshape(key_span, width),
        ],
        axis=1,
    )
    block_rows = row_count * lax.axis_size("group")
    holder = jnp.zeros((block_rows + 2 * LMAX, 2 * width), jnp.float32)
    holder = lax.dynamic_update_slice_in_dim(
        holder, grad_window, lax.axis_index("group") * row_count, 0
    )
    rim_rows = jnp.concatenate([holder[:LMAX], holder[block_rows + LMAX :]], axis=0)
    moved = extended(rim_rows.astype(jnp.bfloat16), (("dp", 0),), LMAX).astype(rim_rows.dtype)
    centre = holder[LMAX : LMAX + block_rows]
    centre = centre.at[:LMAX].add(moved[:LMAX])
    centre = centre.at[block_rows - LMAX :].add(moved[3 * LMAX :])
    pair_grad = lax.psum_scatter(
        centre.astype(jnp.bfloat16), "group", scatter_dimension=0, tiled=True
    ).astype(jnp.float32)
    query_back = rotate(grad_queries, cosine, sine_table, -1.0).reshape(row_count, width)
    key_back = rotate(
        pair_grad[:, :width].reshape(row_count, heads, HEAD_DIM), cosine, sine_table, -1.0
    )
    grad_joined = jnp.concatenate(
        [query_back, key_back.reshape(row_count, width), pair_grad[:, width:]], axis=1
    ).astype(jnp.bfloat16)
    joined_local = jnp.einsum(
        "rd,re->de", normed_in, grad_joined, preferred_element_type=jnp.float32
    )
    grad_normed = jnp.einsum(
        "re,de->rd", grad_joined, joined_half, preferred_element_type=jnp.float32
    )
    gain_one_local = jnp.sum(grad_normed * normed_one, axis=0)
    stream_grad = grad_resid + norm_back(grad_normed * gain_one, normed_one, scale_one)
    locals_all = (joined_local, out_local, wide_local, down_local, gain_one_local, gain_two_local)
    summed = (
        lax.psum_scatter(locals_all[0], ("dp", "group"), scatter_dimension=0, tiled=True),
        lax.psum_scatter(locals_all[1], ("dp", "group"), scatter_dimension=0, tiled=True),
        lax.psum_scatter(locals_all[2], ("dp", "group"), scatter_dimension=0, tiled=True),
        lax.psum_scatter(locals_all[3], ("dp", "group"), scatter_dimension=0, tiled=True),
        lax.psum_scatter(locals_all[4], ("dp", "group"), scatter_dimension=0, tiled=True),
        lax.psum_scatter(locals_all[5], ("dp", "group"), scatter_dimension=0, tiled=True),
    )
    joined_grad, out_grad, wide_grad, down_grad, gain_first_grad, gain_second_grad = summed
    joined_new, joined_momentum_new, joined_variance_new = adam_step(
        joined_proj, joined_grad, joined_momentum, joined_variance, WEIGHT_DECAY
    )
    out_new, out_momentum_new, out_variance_new = adam_step(
        out_proj, out_grad, out_momentum, out_variance, WEIGHT_DECAY
    )
    wide_new, wide_momentum_new, wide_variance_new = adam_step(
        wide_proj, wide_grad, wide_momentum, wide_variance, WEIGHT_DECAY
    )
    down_new, down_momentum_new, down_variance_new = adam_step(
        down_proj, down_grad, down_momentum, down_variance, WEIGHT_DECAY
    )
    gain_first_new, gain_first_momentum_new, gain_first_variance_new = adam_step(
        gain_first, gain_first_grad, gain_first_momentum, gain_first_variance, 0.0
    )
    gain_second_new, gain_second_momentum_new, gain_second_variance_new = adam_step(
        gain_second, gain_second_grad, gain_second_momentum, gain_second_variance, 0.0
    )
    return (
        output,
        stream_grad,
        joined_grad,
        out_grad,
        wide_grad,
        down_grad,
        gain_first_grad,
        gain_second_grad,
        joined_new,
        out_new,
        wide_new,
        down_new,
        gain_first_new,
        gain_second_new,
        joined_momentum_new,
        out_momentum_new,
        wide_momentum_new,
        down_momentum_new,
        gain_first_momentum_new,
        gain_second_momentum_new,
        joined_variance_new,
        out_variance_new,
        wide_variance_new,
        down_variance_new,
        gain_first_variance_new,
        gain_second_variance_new,
    )


def solution(mesh):
    placed = (
        P(("dp", "group"), None),
        P(("dp", "group"), None),
        P(("dp", "group"), None),
        P(("dp", "group"), None),
        P(("dp", "group"), None),
        P(("dp", "group"), None),
        P(("dp", "group"), None),
        P(("dp", "group")),
        P(("dp", "group")),
        P(("dp", "group"), None),
        P(("dp", "group"), None),
        P(("dp", "group"), None),
        P(("dp", "group"), None),
        P(("dp", "group")),
        P(("dp", "group")),
        P(("dp", "group"), None),
        P(("dp", "group"), None),
        P(("dp", "group"), None),
        P(("dp", "group"), None),
        P(("dp", "group")),
        P(("dp", "group")),
    )
    return jax.shard_map(
        on_device,
        mesh=mesh,
        in_specs=placed,
        out_specs=(
            P(("dp", "group"), None),
            P(("dp", "group"), None),
            P(("dp", "group"), None),
            P(("dp", "group"), None),
            P(("dp", "group"), None),
            P(("dp", "group"), None),
            P(("dp", "group")),
            P(("dp", "group")),
            P(("dp", "group"), None),
            P(("dp", "group"), None),
            P(("dp", "group"), None),
            P(("dp", "group"), None),
            P(("dp", "group")),
            P(("dp", "group")),
            P(("dp", "group"), None),
            P(("dp", "group"), None),
            P(("dp", "group"), None),
            P(("dp", "group"), None),
            P(("dp", "group")),
            P(("dp", "group")),
            P(("dp", "group"), None),
            P(("dp", "group"), None),
            P(("dp", "group"), None),
            P(("dp", "group"), None),
            P(("dp", "group")),
            P(("dp", "group")),
        ),
        check_vma=False,
    )
```

profile of v0, /device:TPU:0, one launch (start us, length us, event | category | flops | bytes accessed | tf_op | source)
XLA Modules:
  0.0 1633.6 jit_solution(6893613471907662871)
XLA Ops:
  10.7 42.7 %all-reduce.5 = (bf16[1024]{0:T(1024)(128)(2,1)S(1)}, bf16[1024]{0:T(1024)(128)(2,1)S(1)}) all-reduce(bf16[1024]{0:T(1024)(128)(2,1)S(1)} %dynamic-update-slice.4, bf16[1024]{0:T(1024)(128)(2,1)S(1)} %dynamic-update-slice.5), channel_id=1, replica_groups=mesh['dp'=8,'group'=4] {'dp','group'}, use_global_device_ids=true, to_apply=%add | all-reduce | flops 2048 | bytes 8192
  57.9 25.8 %all-gather.6.cloned.1.call-done = bf16[1024,3072]{1,0:T(8,128)(2,1)} async-done(((bf16[32,3072]{1,0:T(8,128)(2,1)}), bf16[1024,3072]{1,0:T(8,128)(2,1)}) %all-gather.6.cloned.1.call-update) | async-done | bytes 6291472 | tf_op jit(solution)/shard_map/all_gather | solution.py:162
  94.8 77.8 %all-gather.8.cloned.1.call-done = bf16[1024,2048]{1,0:T(8,128)(2,1)} async-done(((bf16[256,2048]{1,0:T(8,128)(2,1)}), bf16[1024,2048]{1,0:T(8,128)(2,1)}) %all-gather.8.cloned.1.call-update) | async-done | bytes 4194320 | tf_op jit(solution)/shard_map/all_gather | solution.py:198
  184.0 8.8 fusion.1
  197.5 6.7 copy.107
  204.3 7.1 copy.105
  263.4 69.7 %all-gather.12.cloned.1.call-done = bf16[1024,5248]{1,0:T(8,128)(2,1)} async-done(((bf16[32,5248]{1,0:T(8,128)(2,1)}), bf16[1024,5248]{1,0:T(8,128)(2,1)}) %all-gather.12.cloned.1.call-update) | async-done | bytes 10747920 | tf_op jit(solution)/shard_map/all_gather | solution.py:164
  333.1 8.9 fusion.75
  342.1 59.1 %all-gather.14.cloned.1.call-done = bf16[1024,2624]{1,0:T(8,128)(2,1)} async-done(((bf16[32,2624]{1,0:T(8,128)(2,1)}), bf16[1024,2624]{1,0:T(8,128)(2,1)}) %all-gather.14.cloned.1.call-update) | async-done | bytes 5373968 | tf_op jit(solution)/shard_map/all_gather | solution.py:165
  401.2 8.0 fusion.17
  421.3 6.8 convolution_bitcast_fusion.4
  483.5 11.6 broadcast_in_dim.44
  495.1 13.8 maximum_dynamic-update-slice_fusion
  509.0 9.3 convert.56
  531.4 7.7 fusion.3
  542.2 6.9 convolution_bitcast_fusion
  549.0 11.9 copy.116
  575.5 121.5 %reduce-scatter.8.cloned.1.call-done = bf16[256,2048]{0,1:T(8,128)(2,1)} async-done(((bf16[1024,2048]{0,1:T(8,128)(2,1)}), bf16[256,2048]{0,1:T(8,128)(2,1)}) %reduce-scatter.8.cloned.1.call-update) | async-done | bytes 1048592 | tf_op jit(solution)/shard_map/reduce_scatter | solution.py:281
  706.9 11.0 fusion.18
  723.6 126.6 %reduce-scatter.12.cloned.1.call-done = f32[32,1024]{1,0:T(8,128)} async-done(((f32[1024,1024]{1,0:T(8,128)}), f32[32,1024]{1,0:T(8,128)}) %reduce-scatter.12.cloned.1.call-update) | async-done | bytes 131088 | tf_op jit(solution)/shard_map/reduce_scatter | solution.py:302
  858.3 37.9 %all-reduce.4 = (f32[1024]{0:T(1024)}, f32[1024]{0:T(1024)}) all-reduce(f32[1024]{0:T(1024)S(1)} %get-tuple-element.172, f32[1024]{0:T(1024)S(1)} %copy-done.54), channel_id=7, replica_groups=mesh['dp'=8,'group'=4] {'dp','group'}, use_global_device_ids=true, to_apply=%region_26.27.clone | all-reduce | flops 2048 | bytes 16384
  901.4 98.5 %reduce-scatter.16.cloned.1.call-done = f32[32,2624]{1,0:T(8,128)} async-done(((f32[1024,2624]{1,0:T(8,128)}), f32[32,2624]{1,0:T(8,128)}) %reduce-scatter.16.cloned.1.call-update) | async-done | bytes 335888
  1002.2 158.1 %reduce-scatter.10.cloned.1.call-done = f32[32,3072]{1,0:T(8,128)} async-done(((f32[1024,3072]{1,0:T(8,128)}), f32[32,3072]{1,0:T(8,128)}) %reduce-scatter.10.cloned.1.call-update) | async-done | bytes 393232 | tf_op jit(solution)/shard_map/reduce_scatter | solution.py:301
  1162.8 460.9 %reduce-scatter.14.cloned.1.call-done = f32[32,5248]{1,0:T(8,128)} async-done(((f32[1024,5248]{1,0:T(8,128)}), f32[32,5248]{1,0:T(8,128)}) %reduce-scatter.14.cloned.1.call-update) | async-done | bytes 671760 | tf_op jit(solution)/shard_map/reduce_scatter | solution.py:303
  (304 shorter events, 220.6 us)
Async XLA Ops:
  7.2 76.6 %all-gather.6.cloned.1.call-start = ((), (), s32[]{:S(2)}) async-start(), calls=%async_computation.5 | async-start | bytes 6488064 | tf_op jit(solution)/shard_map/all_gather | solution.py:162
  9.0 163.6 %all-gather.8.cloned.1.call-start = ((), (), s32[]{:S(2)}) async-start(), calls=%async_computation.6 | async-start | bytes 5242880 | tf_op jit(solution)/shard_map/all_gather | solution.py:198
  93.1 167.4 %all-gather.10.cloned.1.call-start = ((), (), s32[]{:S(2)}) async-start(), calls=%async_computation.7 | async-start | bytes 2162688 | tf_op jit(solution)/shard_map/all_gather | solution.py:163
  93.9 239.3 %all-gather.12.cloned.1.call-start = ((), (), s32[]{:S(2)}) async-start(), calls=%async_computation.8 | async-start | bytes 11083776 | tf_op jit(solution)/shard_map/all_gather | solution.py:164
  94.7 306.5 %all-gather.14.cloned.1.call-start = ((), (), s32[]{:S(2)}) async-start(), calls=%async_computation.9 | async-start | bytes 5677056 | tf_op jit(solution)/shard_map/all_gather | solution.py:165
  172.5 9.4 collective-permute-start.1
  173.8 10.2 collective-permute-start
  179.6 517.4 %reduce-scatter.8.cloned.1.call-start = ((), (), s32[]{:S(2)}) async-start(), calls=%async_computation.10 | async-start | bytes 5242880 | tf_op jit(solution)/shard_map/reduce_scatter | solution.py:281
  179.6 236.1 %copy-start.28 = (f32[1024]{0:T(1024)}, f32[1024]{0:T(1024)S(1)}, u32[]{:S(2)}) copy-start(f32[1024]{0:T(1024)S(1)} %convert_element_type.136) | copy-start | bytes 12292
  263.1 152.6 %copy-start.3 = (f32[256,1024]{1,0:T(8,128)}, f32[256,1024]{1,0:T(8,128)S(1)}, u32[]{:S(2)}) copy-start(f32[256,1024]{1,0:T(8,128)S(1)} %get-tuple-element.242) | copy-start | bytes 3145732
  263.1 152.6 %copy-start.46 = (f32[256]{0:T(256)}, f32[256]{0:T(256)S(1)}, u32[]{:S(2)}) copy-start(f32[256]{0:T(256)S(1)} %broadcast_multiply_fusion.5) | copy-start | bytes 3076
  263.4 152.3 %copy-start.48 = (f32[256]{0:T(256)}, f32[256]{0:T(256)S(1)}, u32[]{:S(2)}) copy-start(f32[256]{0:T(256)S(1)} %add_rsqrt_fusion) | copy-start | bytes 3076
  263.4 137.8 %copy-start.10 = (f32[256,1024]{1,0:T(8,128)S(1)}, f32[256,1024]{1,0:T(8,128)}, u32[]{:S(2)}) copy-start(f32[256,1024]{1,0:T(8,128)} %param.30) | copy-start | bytes 3145732
  519.3 8.9 collective-permute-start.2
  521.7 9.7 collective-permute-start.3
  539.1 311.1 %reduce-scatter.12.cloned.1.call-start = ((), (), s32[]{:S(2)}) async-start(), calls=%async_computation.12 | async-start | bytes 4325376 | tf_op jit(solution)/shard_map/reduce_scatter | solution.py:302
  542.1 457.8 %reduce-scatter.16.cloned.1.call-start = ((), (), s32[]{:S(2)}) async-start(), calls=%async_computation.14 | async-start | bytes 11354112
  560.9 599.4 %reduce-scatter.10.cloned.1.call-start = ((), (), s32[]{:S(2)}) async-start(), calls=%async_computation.11 | async-start | bytes 12976128 | tf_op jit(solution)/shard_map/reduce_scatter | solution.py:301
  705.6 918.0 %reduce-scatter.14.cloned.1.call-start = ((), (), s32[]{:S(2)}) async-start(), calls=%async_computation.13 | async-start | bytes 22167552 | tf_op jit(solution)/shard_map/reduce_scatter | solution.py:303
  852.0 148.0 %copy-start.26 = (f32[32,2624]{1,0:T(8,128)S(1)}, f32[32,2624]{1,0:T(8,128)}, u32[]{:S(2)}) copy-start(f32[32,2624]{1,0:T(8,128)} %param.35) | copy-start | bytes 1007620
  858.3 302.1 %copy-start.24 = (f32[32,3072]{1,0:T(8,128)S(1)}, f32[32,3072]{1,0:T(8,128)}, u32[]{:S(2)}) copy-start(f32[32,3072]{1,0:T(8,128)} %param.32) | copy-start | bytes 1179652
  858.3 765.4 %copy-start.13 = (f32[32,5248]{1,0:T(8,128)S(1)}, f32[32,5248]{1,0:T(8,128)}, u32[]{:S(2)}) copy-start(f32[32,5248]{1,0:T(8,128)} %param.34) | copy-start | bytes 2015236
  901.4 722.2 %copy-start.30 = (f32[32,5248]{1,0:T(8,128)S(1)}, f32[32,5248]{1,0:T(8,128)}, u32[]{:S(2)}) copy-start(f32[32,5248]{1,0:T(8,128)} %param.40) | copy-start | bytes 2015236
  901.4 722.2 %copy-start.31 = (f32[32,5248]{1,0:T(8,128)S(1)}, f32[32,5248]{1,0:T(8,128)}, u32[]{:S(2)}) copy-start(f32[32,5248]{1,0:T(8,128)} %param.46) | copy-start | bytes 2015236
  (75 other events, 2021.9 us)
Sparse Core Ops, SparseCore 0:
  11.5 72.2 all-gather.5
  93.2 79.2 all-gather.7
  176.1 58.8 all-gather.9
  238.2 94.9 all-gather.11
  336.4 64.7 all-gather.13
  539.2 157.7 reduce-scatter.7
  699.8 150.3 reduce-scatter.11
  856.8 143.1 reduce-scatter.15
  1006.5 153.7 reduce-scatter.9
  1163.1 460.5 reduce-scatter.13
where the time goes:
time: 1640 us; the launch traced here: 1630 us
  waiting for transfers between devices  1210 us (74%)
  matrix products  167 us (10%)
  other arithmetic  96.8 us (6%)
  blocking collectives  80.6 us (5%)
  local copies, waits for them, and re-layouts  52.9 us (3%)
    reduce_scatter x1, waiting for transfers between devices, on_device(): lax.psum_scatter(locals_all[2], ('dp', 'group'), scatter_dimension=0, til...  461 us
    reduce_scatter x1, waiting for transfers between devices, on_device(): lax.psum_scatter(locals_all[0], ('dp', 'group'), scatter_dimension=0, til...  158 us
    reduce_scatter x1, waiting for transfers between devices, on_device(): lax.psum_scatter(locals_all[1], ('dp', 'group'), scatter_dimension=0, til...  127 us
    reduce_scatter x1, waiting for transfers between devices, on_device(): lax.psum_scatter(centre.astype(jnp.bfloat16), 'group', scatter_dimension=...  121 us
    unnamed x11, waiting for transfers between devices  98.7 us
    unnamed x2, blocking collectives  80.6 us
    all_gather x1, waiting for transfers between devices, on_device(): group_block = lax.all_gather(pairs, 'group', axis=0, tiled=True)  77.8 us
    all_gather x1, waiting for transfers between devices, on_device(): lax.all_gather(masters[2], ('dp', 'group'), axis=0, tiled=True)  69.7 us
  transfers between devices with their start and end apart: 14, of which 13 were waited for; matrix products, arithmetic and copies ran while one was open for 11% of the time, Pallas kernels for 0%

commit v1 on v0

--- a/solution.py
+++ b/solution.py
@@ -8,6 +8,8 @@
 HEAD_DIM = 64
 LMAX = 1024
 STEP = 4
+GAIN_PAD = 384
+OUT_PAD = 128
 
 
 EPSILON = 1e-05
@@ -122,6 +124,16 @@
         / (jnp.sqrt(new_variance / (1.0 - BETA_TWO**STEP)) + ADAM_EPSILON)
     )
     return (weight - LEARN_RATE * (update + decay_rate * weight), new_momentum, new_variance)
+
+
+def scatter_sum(partial):
+    moved = partial.astype(jnp.bfloat16)
+    total = lax.psum_scatter(moved, ("dp", "group"), scatter_dimension=0, tiled=True)
+    return total.astype(jnp.float32)
+
+
+def with_column(matrix, column, extra):
+    return jnp.concatenate([matrix, jnp.pad(column[:, None], ((0, 0), (0, extra - 1)))], axis=1)
 
 
 def on_device(
@@ -150,23 +162,17 @@
     row_count = stream.shape[0]
     width = stream.shape[1]
     heads = width // HEAD_DIM
-    masters = (
-        joined_proj.astype(jnp.bfloat16),
-        out_proj.astype(jnp.bfloat16),
-        wide_proj.astype(jnp.bfloat16),
-        down_proj.astype(jnp.bfloat16),
-        gain_first.astype(jnp.bfloat16),
-        gain_second.astype(jnp.bfloat16),
-    )
-    gathered = (
-        lax.all_gather(masters[0], ("dp", "group"), axis=0, tiled=True),
-        lax.all_gather(masters[1], ("dp", "group"), axis=0, tiled=True),
-        lax.all_gather(masters[2], ("dp", "group"), axis=0, tiled=True),
-        lax.all_gather(masters[3], ("dp", "group"), axis=0, tiled=True),
-        lax.all_gather(masters[4], ("dp", "group"), axis=0, tiled=True),
-        lax.all_gather(masters[5], ("dp", "group"), axis=0, tiled=True),
-    )
-    joined_half, out_half, wide_half, down_half, gain_one_half, gain_two_half = gathered
+    both = ("dp", "group")
+    gains = jnp.stack([gain_first, gain_second], axis=1)
+    gains = jnp.pad(gains, ((0, 0), (0, GAIN_PAD - 2)))
+    joined_gains = jnp.concatenate([joined_proj, gains], axis=1).astype(jnp.bfloat16)
+    joined_gains = lax.all_gather(joined_gains, both, axis=0, tiled=True)
+    joined_half = joined_gains[:, : 3 * width]
+    gain_one_half = joined_gains[:, 3 * width]
+    gain_two_half = joined_gains[:, 3 * width + 1]
+    out_half = lax.all_gather(out_proj.astype(jnp.bfloat16), both, axis=0, tiled=True)
+    wide_half = lax.all_gather(wide_proj.astype(jnp.bfloat16), both, axis=0, tiled=True)
+    down_half = lax.all_gather(down_proj.astype(jnp.bfloat16), both, axis=0, tiled=True)
     gain_one = gain_one_half.astype(jnp.float32)
     gain_two = gain_two_half.astype(jnp.float32)
     ff_width = down_half.shape[1]
@@ -230,15 +236,22 @@
     cot_half = cotangent.astype(jnp.bfloat16)
     down_local = jnp.einsum("rd,rf->df", cot_half, gated, preferred_element_type=jnp.float32)
     grad_gated = jnp.dot(cot_half, down_half, preferred_element_type=jnp.float32)
-    grad_wide = jnp.concatenate(
-        [grad_gated * gate_part * gelu_slope, grad_gated * activation], axis=1
-    ).astype(jnp.bfloat16)
-    wide_local = jnp.einsum("rd,rf->df", hidden_in, grad_wide, preferred_element_type=jnp.float32)
+    grad_inner = (grad_gated * gate_part * gelu_slope).astype(jnp.bfloat16)
+    grad_gate = (grad_gated * activation).astype(jnp.bfloat16)
+    grad_wide = jnp.concatenate([grad_inner, grad_gate], axis=1)
+    down_sum = scatter_sum(down_local)
+    inner_sum = scatter_sum(
+        jnp.einsum("rd,rf->df", hidden_in, grad_inner, preferred_element_type=jnp.float32)
+    )
+    gate_sum = scatter_sum(
+        jnp.einsum("rd,rf->df", hidden_in, grad_gate, preferred_element_type=jnp.float32)
+    )
     grad_hidden = jnp.einsum("rf,df->rd", grad_wide, wide_half, preferred_element_type=jnp.float32)
     gain_two_local = jnp.sum(grad_hidden * normed_two, axis=0)
     grad_resid = cotangent + norm_back(grad_hidden * gain_two, normed_two, scale_two)
     resid_half = grad_resid.astype(jnp.bfloat16)
     out_local = jnp.einsum("rd,re->de", attended, resid_half, preferred_element_type=jnp.float32)
+    out_sum = scatter_sum(with_column(out_local, gain_two_local, OUT_PAD))
     grad_attended = jnp.einsum(
         "re,de->rd", resid_half, out_half, preferred_element_type=jnp.float32
     ).astype(jnp.bfloat16)
@@ -269,13 +282,13 @@
         axis=1,
     )
     block_rows = row_count * lax.axis_size("group")
-    holder = jnp.zeros((block_rows + 2 * LMAX, 2 * width), jnp.float32)
+    holder = jnp.zeros((block_rows + 2 * LMAX, 2 * width), jnp.bfloat16)
     holder = lax.dynamic_update_slice_in_dim(
-        holder, grad_window, lax.axis_index("group") * row_count, 0
+        holder, grad_window.astype(jnp.bfloat16), lax.axis_index("group") * row_count, 0
     )
     rim_rows = jnp.concatenate([holder[:LMAX], holder[block_rows + LMAX :]], axis=0)
-    moved = extended(rim_rows.astype(jnp.bfloat16), (("dp", 0),), LMAX).astype(rim_rows.dtype)
-    centre = holder[LMAX : LMAX + block_rows]
+    moved = extended(rim_rows, (("dp", 0),), LMAX).astype(jnp.float32)
+    centre = holder[LMAX : LMAX + block_rows].astype(jnp.float32)
     centre = centre.at[:LMAX].add(moved[:LMAX])
     centre = centre.at[block_rows - LMAX :].add(moved[3 * LMAX :])
     pair_grad = lax.psum_scatter(
@@ -296,16 +309,13 @@
     )
     gain_one_local = jnp.sum(grad_normed * normed_one, axis=0)
     stream_grad = grad_resid + norm_back(grad_normed * gain_one, normed_one, scale_one)
-    locals_all = (joined_local, out_local, wide_local, down_local, gain_one_local, gain_two_local)
-    summed = (
-        lax.psum_scatter(locals_all[0], ("dp", "group"), scatter_dimension=0, tiled=True),
-        lax.psum_scatter(locals_all[1], ("dp", "group"), scatter_dimension=0, tiled=True),
-        lax.psum_scatter(locals_all[2], ("dp", "group"), scatter_dimension=0, tiled=True),
-        lax.psum_scatter(locals_all[3], ("dp", "group"), scatter_dimension=0, tiled=True),
-        lax.psum_scatter(locals_all[4], ("dp", "group"), scatter_dimension=0, tiled=True),
-        lax.psum_scatter(locals_all[5], ("dp", "group"), scatter_dimension=0, tiled=True),
-    )
-    joined_grad, out_grad, wide_grad, down_grad, gain_first_grad, gain_second_grad = summed
+    joined_sum = scatter_sum(with_column(joined_local, gain_one_local, GAIN_PAD))
+    joined_grad = joined_sum[:, : 3 * width]
+    gain_first_grad = joined_sum[:, 3 * width]
+    out_grad = out_sum[:, :width]
+    gain_second_grad = out_sum[:, width]
+    wide_grad = jnp.concatenate([inner_sum, gate_sum], axis=1)
+    down_grad = down_sum
     joined_new, joined_momentum_new, joined_variance_new = adam_step(
         joined_proj, joined_grad, joined_momentum, joined_variance, WEIGHT_DECAY
     )

time: 1640 us -> 1280 us (0.78)
  waiting for transfers between devices: 1210 us -> 947 us
  blocking collectives: 80.6 us -> 0 us
    reduce_scatter x3 -> x5, waiting for transfers between devices: 746 us -> 543 us  [scatter_sum(): lax.psum_scatter(moved, ('dp', 'group'), scatter_dimension=0, tiled=True)]
    unnamed x11, waiting for transfers between devices: 98.7 us -> 0.19 us
    unnamed x2 -> x0, blocking collectives: 80.6 us -> none
    all_gather x4, waiting for transfers between devices: 155 us -> 206 us  [the longest x1 75.1 us: on_device(): lax.all_gather(wide_proj.astype(jnp.bfloat16), both, axis=0, tiled=True)]
  transfers between devices with their start and end apart: 14 -> 15, of which waited for: 13 -> 14; matrix products, arithmetic and copies ran while one was open for 11% -> 13% of each run, Pallas kernels for 0% -> 0%
where the time goes in v1:
time: 1280 us; the launch traced here: 1270 us
  waiting for transfers between devices  947 us (74%)
  matrix products  165 us (13%)
  other arithmetic  82.6 us (6%)
  local copies, waits for them, and re-layouts  50.6 us (4%)
  between operations  15.4 us (1%)
    reduce_scatter x5, waiting for transfers between devices, scatter_sum(): lax.psum_scatter(moved, ('dp', 'group'), scatter_dimension=0, tiled=True)  543 us
    reduce_scatter x1, waiting for transfers between devices, on_device(): lax.psum_scatter(centre.astype(jnp.bfloat16), 'group', scatter_dimension=...  109 us
    all_gather x1, waiting for transfers between devices, on_device(): group_block = lax.all_gather(pairs, 'group', axis=0, tiled=True)  77.8 us
    all_gather x1, waiting for transfers between devices, on_device(): lax.all_gather(wide_proj.astype(jnp.bfloat16), both, axis=0, tiled=True)  75.1 us
    all_gather x1, waiting for transfers between devices, on_device(): joined_gains = lax.all_gather(joined_gains, both, axis=0, tiled=True)  71.9 us
    all_gather x1, waiting for transfers between devices, on_device(): lax.all_gather(down_proj.astype(jnp.bfloat16), both, axis=0, tiled=True)  58.7 us
  transfers between devices with their start and end apart: 15, of which 14 were waited for; matrix products, arithmetic and copies ran while one was open for 13% of the time, Pallas kernels for 0%

profile of v1, /device:TPU:0, one launch (start us, length us, event | category | flops | bytes accessed | tf_op | source)
XLA Modules:
  0.0 1271.7 jit_solution(12521808325152446128)
XLA Ops:
  14.3 71.9 %all-gather.6.cloned.1.call-done = bf16[1024,3456]{1,0:T(8,128)(2,1)} async-done(((bf16[32,3456]{1,0:T(8,128)(2,1)}), bf16[1024,3456]{1,0:T(8,128)(2,1)}) %all-gather.6.cloned.1.call-update) | async-done | bytes 7077904 | tf_op jit(solution)/shard_map/all_gather | solution.py:169
  98.5 77.8 %all-gather.8.cloned.1.call-done = bf16[1024,2048]{1,0:T(8,128)(2,1)} async-done(((bf16[256,2048]{1,0:T(8,128)(2,1)}), bf16[1024,2048]{1,0:T(8,128)(2,1)}) %all-gather.8.cloned.1.call-update) | async-done | bytes 4194320 | tf_op jit(solution)/shard_map/all_gather | solution.py:204
  187.8 8.8 fusion.2
  201.3 6.8 copy.149
  208.1 7.0 copy.147
  251.1 6.1 fusion.62
  261.9 75.1 %all-gather.12.cloned.1.call-done = bf16[1024,5248]{1,0:T(8,128)(2,1)} async-done(((bf16[32,5248]{1,0:T(8,128)(2,1)}), bf16[1024,5248]{1,0:T(8,128)(2,1)}) %all-gather.12.cloned.1.call-update) | async-done | bytes 10747920 | tf_op jit(solution)/shard_map/all_gather | solution.py:174
  336.9 9.3 fusion.107
  346.3 58.7 %all-gather.14.cloned.1.call-done = bf16[1024,2624]{1,0:T(8,128)(2,1)} async-done(((bf16[32,2624]{1,0:T(8,128)(2,1)}), bf16[1024,2624]{1,0:T(8,128)(2,1)}) %all-gather.14.cloned.1.call-update) | async-done | bytes 5373968 | tf_op jit(solution)/shard_map/all_gather | solution.py:175
  405.0 8.5 fusion.33
  427.9 6.6 fusion.20
  434.5 6.4 fusion.23
  443.6 6.6 fusion.21
  450.2 7.0 multiply_convert_fusion.3
  490.4 6.2 broadcast_in_dim.50
  496.6 8.9 maximum_dynamic-update-slice_fusion
  541.1 8.0 copy.159
  576.0 109.3 %reduce-scatter.11.cloned.1.call-done = bf16[256,2048]{0,1:T(8,128)(2,1)} async-done(((bf16[1024,2048]{0,1:T(8,128)(2,1)}), bf16[256,2048]{0,1:T(8,128)(2,1)}) %reduce-scatter.11.cloned.1.call-update) | async-done | bytes 1048592 | tf_op jit(solution)/shard_map/reduce_scatter | solution.py:294
  688.4 6.3 multiply_reduce_fusion.1
  706.2 84.7 %reduce-scatter.19.cloned.1.call-done = bf16[32,1152]{1,0:T(8,128)(2,1)} async-done(((bf16[1024,1152]{1,0:T(8,128)(2,1)}), bf16[32,1152]{1,0:T(8,128)(2,1)}) %reduce-scatter.19.cloned.1.call-update) | async-done | bytes 73744 | tf_op jit(solution)/shard_map/reduce_scatter | solution.py:131
  794.3 112.0 %reduce-scatter.21.cloned.1.call-done = bf16[32,2624]{1,0:T(8,128)(2,1)} async-done(((bf16[1024,2624]{1,0:T(8,128)(2,1)}), bf16[32,2624]{1,0:T(8,128)(2,1)}) %reduce-scatter.21.cloned.1.call-update) | async-done | bytes 167952 | tf_op jit(solution)/shard_map/reduce_scatter | solution.py:131
  908.6 113.0 %reduce-scatter.15.cloned.1.call-done = bf16[32,2624]{1,0:T(8,128)(2,1)} async-done(((bf16[1024,2624]{1,0:T(8,128)(2,1)}), bf16[32,2624]{1,0:T(8,128)(2,1)}) %reduce-scatter.15.cloned.1.call-update) | async-done | bytes 167952 | tf_op jit(solution)/shard_map/reduce_scatter | solution.py:131
  1021.6 115.1 %reduce-scatter.17.cloned.1.call-done = bf16[32,2624]{1,0:T(8,128)(2,1)} async-done(((bf16[1024,2624]{1,0:T(8,128)(2,1)}), bf16[32,2624]{1,0:T(8,128)(2,1)}) %reduce-scatter.17.cloned.1.call-update) | async-done | bytes 167952 | tf_op jit(solution)/shard_map/reduce_scatter | solution.py:131
  1142.8 118.1 %reduce-scatter.13.cloned.1.call-done = bf16[32,3456]{1,0:T(8,128)(2,1)} async-done(((bf16[1024,3456]{1,0:T(8,128)(2,1)}), bf16[32,3456]{1,0:T(8,128)(2,1)}) %reduce-scatter.13.cloned.1.call-update) | async-done | bytes 221200 | tf_op jit(solution)/shard_map/reduce_scatter | solution.py:131
  (284 shorter events, 218.3 us)
Async XLA Ops:
  7.2 79.1 %all-gather.6.cloned.1.call-start = ((), (), s32[]{:S(2)}) async-start(), calls=%async_computation.6 | async-start | bytes 7299072 | tf_op jit(solution)/shard_map/all_gather | solution.py:169
  9.8 166.6 %all-gather.8.cloned.1.call-start = ((), (), s32[]{:S(2)}) async-start(), calls=%async_computation.7 | async-start | bytes 5242880 | tf_op jit(solution)/shard_map/all_gather | solution.py:204
  96.9 162.1 %all-gather.10.cloned.1.call-start = ((), (), s32[]{:S(2)}) async-start(), calls=%async_computation.8 | async-start | bytes 2162688 | tf_op jit(solution)/shard_map/all_gather | solution.py:173
  97.6 239.3 %all-gather.12.cloned.1.call-start = ((), (), s32[]{:S(2)}) async-start(), calls=%async_computation.9 | async-start | bytes 11083776 | tf_op jit(solution)/shard_map/all_gather | solution.py:174
  98.5 306.5 %all-gather.14.cloned.1.call-start = ((), (), s32[]{:S(2)}) async-start(), calls=%async_computation.10 | async-start | bytes 5677056 | tf_op jit(solution)/shard_map/all_gather | solution.py:175
  176.4 9.4 collective-permute-start.1
  177.6 10.2 collective-permute-start
  183.3 502.0 %reduce-scatter.11.cloned.1.call-start = ((), (), s32[]{:S(2)}) async-start(), calls=%async_computation.11 | async-start | bytes 5242880 | tf_op jit(solution)/shard_map/reduce_scatter | solution.py:294
  509.4 8.9 collective-permute-start.2
  511.8 9.6 collective-permute-start.3
  527.5 263.4 %reduce-scatter.19.cloned.1.call-start = ((), (), s32[]{:S(2)}) async-start(), calls=%async_computation.15 | async-start | bytes 2433024 | tf_op jit(solution)/shard_map/reduce_scatter | solution.py:131
  535.5 370.8 %reduce-scatter.21.cloned.1.call-start = ((), (), s32[]{:S(2)}) async-start(), calls=%async_computation.16 | async-start | bytes 5677056 | tf_op jit(solution)/shard_map/reduce_scatter | solution.py:131
  549.1 472.5 %reduce-scatter.15.cloned.1.call-start = ((), (), s32[]{:S(2)}) async-start(), calls=%async_computation.13 | async-start | bytes 5677056 | tf_op jit(solution)/shard_map/reduce_scatter | solution.py:131
  554.7 582.0 %reduce-scatter.17.cloned.1.call-start = ((), (), s32[]{:S(2)}) async-start(), calls=%async_computation.14 | async-start | bytes 5677056 | tf_op jit(solution)/shard_map/reduce_scatter | solution.py:131
  560.3 700.6 %reduce-scatter.13.cloned.1.call-start = ((), (), s32[]{:S(2)}) async-start(), calls=%async_computation.12 | async-start | bytes 7299072 | tf_op jit(solution)/shard_map/reduce_scatter | solution.py:131
  700.4 205.9 %copy-start.12 = (f32[32,2624]{1,0:T(8,128)S(1)}, f32[32,2624]{1,0:T(8,128)}, u32[]{:S(2)}) copy-start(f32[32,2624]{1,0:T(8,128)} %param.35) | copy-start | bytes 1007620
  706.2 434.1 %copy-start.41 = (f32[256]{0:T(256)S(1)}, f32[256]{0:T(256)}, u32[]{:S(2)}) copy-start(f32[256]{0:T(256)} %get-tuple-element.149) | copy-start | bytes 3076
  791.9 350.9 %copy-start.37 = (f32[32]{0:T(128)}, f32[32]{0:T(128)S(1)}, u32[]{:S(2)}) copy-start(f32[32]{0:T(128)S(1)} %slice_reduce_fusion) | copy-start | bytes 388
  908.5 353.5 %copy-start.40 = (f32[32]{0:T(128)S(1)}, f32[32]{0:T(128)}, u32[]{:S(2)}) copy-start(f32[32]{0:T(128)} %param.36) | copy-start | bytes 388
  908.5 353.5 %copy-start.44 = (f32[32]{0:T(128)S(1)}, f32[32]{0:T(128)}, u32[]{:S(2)}) copy-start(f32[32]{0:T(128)} %param.42) | copy-start | bytes 388
  908.6 353.5 %copy-start.45 = (f32[32]{0:T(128)S(1)}, f32[32]{0:T(128)}, u32[]{:S(2)}) copy-start(f32[32]{0:T(128)} %param.48) | copy-start | bytes 388
  908.6 354.0 %copy-start.10 = (f32[32,3072]{1,0:T(8,128)S(1)}, f32[32,3072]{1,0:T(8,128)}, u32[]{:S(2)}) copy-start(f32[32,3072]{1,0:T(8,128)} %param.32) | copy-start | bytes 1179652
  908.6 354.0 %copy-start.22 = (f32[32,3072]{1,0:T(8,128)S(1)}, f32[32,3072]{1,0:T(8,128)}, u32[]{:S(2)}) copy-start(f32[32,3072]{1,0:T(8,128)} %param.38) | copy-start | bytes 1179652
  908.6 354.0 %copy-start.23 = (f32[32,3072]{1,0:T(8,128)S(1)}, f32[32,3072]{1,0:T(8,128)}, u32[]{:S(2)}) copy-start(f32[32,3072]{1,0:T(8,128)} %param.44) | copy-start | bytes 1179652
  (62 other events, 1587.9 us)
Sparse Core Ops, SparseCore 0:
  11.4 74.8 all-gather.5
  97.0 79.2 all-gather.7
  179.9 58.8 all-gather.9
  242.0 94.9 all-gather.11
  340.2 64.7 all-gather.13
  527.6 157.7 reduce-scatter.10
  690.7 100.1 reduce-scatter.18
  796.4 109.7 reduce-scatter.20
  911.8 109.7 reduce-scatter.14
  1027.0 109.6 reduce-scatter.16
  1142.4 118.4 reduce-scatter.12
